TPU v7x, 32 devices: a whole 2x2x4 slice. The times are simulated.
32 devices in a mesh: group: 4 (over y, x), shard: 8 (over z, core).
Axes of the slice: x: 2, y: 2, z: 4, core: 2. Of those that a mesh axis runs over, the one named last changes fastest.
Arguments:
- queries: float32 [256, 768], P(('group', 'shard')), may hold values from -6 to 6
- codebook: float32 [96, 256, 8], replicated, may hold values from -0.21875 to 0.21875
- pq_codes: int32 [256, 96, 256], P(('group', 'shard')), may hold values from 0 to 255
- probes: int32 [256, 8], P('group'), may hold values from 0 to 63, all different within a row
- vectors: float32 [32768, 768], P(('group', 'shard')), may hold values from -0.21875 to 0.21875
- cand_owner: int32 [256, 16], P(('group', 'shard')), may hold values from 0 to 31, all different within a row; in each aligned block of 8 rows (0 to 7, 8 to 15, ...) at most 4 rows name the same one
- cand_row: int32 [256, 16], P(('group', 'shard')), may hold values from 0 to 1023
Outputs:
- pq_scores: float32 [256, 256, 64], P(('group', 'shard'))
- rerank_scores: float32 [256, 16], P(('group', 'shard'))
Inputs may be any that keep to these rules, and one draw needn't show every extreme that they name: The 8 probes of one query are distinct. `cand_owner`: the 16 owners of one query are distinct. Among the queries of one device no owner appears more than 4 times, and some owner appears exactly 4 times.
All inputs are finite; a program needn't handle non-finite values.
Results may differ from a plain program's by a relative error of at most 0.0029.
Values may be sent and summed in bfloat16 or wider, within the bound.
No kernel may reach another device: no remote copies, remote signals or barrier semaphores. Data moves between devices by JAX's collectives and lax.ppermute only.
A program may use at most 128 MiB of HBM per device.

v0:
```python
import jax
import jax.numpy as jnp
from jax import lax
from jax.sharding import PartitionSpec as P

M = 96
DS = 8
KS = 256


def build_tables(query_rows, codebook):
    number = query_rows.shape[0]
    pieces = query_rows.reshape(number, M, DS)
    tables = jnp.einsum("qmd,mkd->qmk", pieces, codebook, precision=lax.Precision.HIGHEST)
    return tables.reshape(number, M * KS).astype(jnp.bfloat16)


def score_lists(pq_codes, group_tables, probes, first_list):
    centres = jnp.arange(KS, dtype=jnp.int32)

    def one_list(inputs):
        list_codes, list_id = inputs
        onehot = (list_codes[:, None, :] == centres[None, :, None]).astype(jnp.bfloat16)
        onehot = onehot.reshape(M * KS, list_codes.shape[1])
        scores = lax.dot_general(
            onehot, group_tables, (((0,), (1,)), ((), ())), preferred_element_type=jnp.float32
        )
        probed = jnp.any(probes == list_id, axis=1)
        return jnp.where(probed[None, :], scores, 0.0)

    list_ids = first_list + jnp.arange(pq_codes.shape[0], dtype=jnp.int32)
    return lax.map(one_list, (pq_codes, list_ids))


def rerank(queries, vectors, cand_owner, cand_row):
    owners = lax.axis_size("group") * lax.axis_size("shard")
    pair_count = cand_owner.shape[0] * cand_owner.shape[1]
    capacity = max(2, pair_count // owners)
    owner_flat = cand_owner.reshape(pair_count)
    matches = (owner_flat[:, None] == jnp.arange(owners, dtype=jnp.int32)[None, :]).astype(
        jnp.int32
    )
    before = jnp.cumsum(matches, axis=0) - matches
    position = jnp.sum(before * matches, axis=1)
    target = owner_flat * capacity + position
    source = jnp.arange(pair_count, dtype=jnp.int32) // cand_owner.shape[1]
    send_rows = (
        jnp.zeros((owners * capacity, queries.shape[1]), jnp.float32)
        .at[target]
        .set(queries[source])
    )
    send_rows = send_rows.reshape(owners, capacity, queries.shape[1])
    send_ids = (
        jnp.full((owners * capacity,), -1.0, jnp.float32)
        .at[target]
        .set(cand_row.reshape(pair_count).astype(jnp.float32))
    )
    send_ids = send_ids.reshape(owners, capacity)
    rows_in = lax.all_to_all(send_rows, ("group", "shard"), split_axis=0, concat_axis=0, tiled=True)
    row_ids = lax.all_to_all(send_ids, ("group", "shard"), split_axis=0, concat_axis=0, tiled=True)
    filled = row_ids >= 0.0
    lookup = jnp.maximum(row_ids, 0.0).astype(jnp.int32)
    found = vectors[lookup]
    inner = jnp.einsum("snd,snd->sn", rows_in, found, precision=lax.Precision.HIGHEST)
    scored = jnp.where(filled, inner, 0.0)
    returned = lax.all_to_all(scored, ("group", "shard"), split_axis=0, concat_axis=0, tiled=True)
    result = returned.reshape(owners * capacity)[target]
    return result.reshape(cand_owner.shape)


def per_device(queries, codebook, pq_codes, probes, vectors, cand_owner, cand_row):
    first_list = lax.axis_index("shard") * pq_codes.shape[0]
    group_queries = lax.all_gather(queries, "shard", axis=0, tiled=True)
    group_tables = build_tables(group_queries, codebook)
    pq_scores = score_lists(pq_codes, group_tables, probes, first_list)
    rerank_scores = rerank(queries, vectors, cand_owner, cand_row)
    return (pq_scores, rerank_scores)


def solution(mesh):
    in_specs = (
        P(("group", "shard"), None),
        P(),
        P(("group", "shard"), None, None),
        P("group", None),
        P(("group", "shard"), None),
        P(("group", "shard"), None),
        P(("group", "shard"), None),
    )
    out_specs = (P(("group", "shard"), None, None), P(("group", "shard"), None))
    return jax.shard_map(
        per_device, mesh=mesh, in_specs=in_specs, out_specs=out_specs, check_vma=False
    )
```

profile of v0, /device:TPU:0, one launch (start us, length us, event | category | flops | bytes accessed | tf_op | source)
XLA Modules:
  0.0 161.3 jit_solution(348428554868212641)
XLA Ops:
  0.6 0.8 broadcast_multiply_fusion
  1.5 0.9 eq.43
  2.9 0.7 convert_element_type.36
  3.7 1.0 scatter_custom_fusion
  4.7 0.7 all_to_all.15
  5.4 7.5 %all-to-all-start = ((f32[32,1,4]{2,1,0:T(1,128)}), f32[32,1,4]{2,1,0:T(1,128)}, u32[]{:S(2)}, u32[]{:S(2)}) async-start(f32[32,1,4]{2,1,0:T(1,128)} %bitcast.4), calls=%async_computation | async-start | bytes 32768 | tf_op jit(solution)/shard_map/all_to_all | solution.py:60
  12.8 15.7 %all_gather.3 = f32[64,768]{1,0:T(8,128)} all-gather(f32[8,768]{1,0:T(8,128)} %param.9), channel_id=1, replica_groups=mesh['group'=4,'shard'=8] {'shard'}, dimensions={0}, use_global_device_ids=true | all-gather | bytes 221184 | tf_op jit(solution)/shard_map/all_gather | solution.py:73
  28.6 1.1 copy.27
  29.7 7.5 %convert_bitcast_fusion = bf16[96,8,8,256]{3,2,1,0:T(8,128)(2,1)} fusion(f32[96,256,8]{1,2,0:T(8,128)} %param.10, f32[64,768]{0,1:T(8,128)S(1)} %copy.27), kind=kOutput, calls=%fused_computation.13 | convolution fusion | flops 152567808 | bytes 4128768 | tf_op jit(solution)/shard_map/qmd,mkd->qmk/dot_general | solution.py:14
  37.2 3.8 %copy.40 = bf16[96,8,8,256]{3,2,0,1:T(8,128)(2,1)} copy(bf16[96,8,8,256]{3,2,1,0:T(8,128)(2,1)} %convert_bitcast_fusion) | data formatting | bytes 6291456 | tf_op jit(solution)/shard_map/convert_element_type | solution.py:15
  41.0 3.0 %scatter_custom_fusion.1 = f32[128,768]{1,0:T(8,128)S(1)} fusion(s32[128]{0:T(128)S(1)} %fusion.10, f32[8,768]{1,0:T(8,128)} %param.9, s32[1024]{0:T(1024)S(1)} %pad_clamp_fusion.2, f32[]{:T(128)} %constant.28.clone.1), kind=kCustom, calls=%fused_computation.16 | custom fusion | bytes 393728 | tf_op jit(solution)/shard_map/scatter | solution.py:50
  44.0 0.9 reshape.135
  44.8 5.4 %all-to-all-start.1 = ((f32[32,4,768]{2,1,0:T(4,128)}), f32[32,4,768]{2,1,0:T(4,128)S(1)}, u32[]{:S(2)}, u32[]{:S(2)}) async-start(f32[32,4,768]{2,1,0:T(4,128)} %reshape.135), calls=%async_computation.1 | async-start | bytes 786432 | tf_op jit(solution)/shard_map/all_to_all | solution.py:59
  50.3 84.8 %while.11 = (s32[]{:T(128)}, f32[8,256,64]{1,2,0:T(8,128)}, s32[8]{0:T(128)S(1)}, s32[64,8]{0,1:T(8,128)S(1)}, s32[8,96,256]{2,1,0:T(8,128)}, /*index=5*/bf16[64,24576]{1,0:T(8,128)(2,1)}, s32[]{:T(128)}) while((s32[]{:T(128)}, f32[8,256,64]{1,2,0:T(8,128)}, s32[8]{0:T(128)S(1)}, s32[64,8]{0,1:T(8,128)S(1)}, ...), condition=%wide.region_2.3_spmd.clone, body=%wide.region_0.2_spmd.clone.sunk | while | flops 811615168 | bytes 29067528 | solution.py:32
  50.4 1.1 dynamic-slice_bitcast_fusion.2
  51.5 4.3 %bitcast_compare_fusion.2 = pred[24576,256]{1,0:T(32,128)(4,1)S(1)} fusion(s32[24576]{0:T(1024)S(1)} %bitcast.56, s32[96,256]{1,0:T(8,128)S(1)} %dynamic-slice_bitcast_fusion.2), kind=kLoop, calls=%fused_computation.6.clone.1 | loop fusion | flops 6291456 | bytes 6488064 | tf_op jit(solution)/shard_map/while/body/eval_jaxpr/eq | solution.py:23
  57.0 3.9 %fusion.21 = f32[8,256,64]{1,2,0:T(8,128)} fusion(f32[8,256,64]{1,2,0:T(8,128)} %get-tuple-element.111, s32[]{:T(128)S(6)} %copy.46, pred[24576,256]{1,0:T(32,128)(4,1)S(1)} %bitcast_compare_fusion.2, bf16[64,24576]{1,0:T(8,128)(2,1)S(1)} %copy-done.1, pred[64]{0:T(512)(128)(4,1)S(1)} %compare_reduce_fusion.2), kind=kOutput, calls=%fused_computation.9.clone.1 | convolution fusion | flops 805322752 | bytes 9502788 | tf_op jit(solution)/shard_map/while/body/eval_jaxpr/dot_general | solution.py:25
  61.0 1.1 dynamic-slice_bitcast_fusion.2
  62.1 4.3 %bitcast_compare_fusion.2 = pred[24576,256]{1,0:T(32,128)(4,1)S(1)} fusion(s32[24576]{0:T(1024)S(1)} %bitcast.56, s32[96,256]{1,0:T(8,128)S(1)} %dynamic-slice_bitcast_fusion.2), kind=kLoop, calls=%fused_computation.6.clone.1 | loop fusion | flops 6291456 | bytes 6488064 | tf_op jit(solution)/shard_map/while/body/eval_jaxpr/eq | solution.py:23
  67.6 3.9 %fusion.21 = f32[8,256,64]{1,2,0:T(8,128)} fusion(f32[8,256,64]{1,2,0:T(8,128)} %get-tuple-element.111, s32[]{:T(128)S(6)} %copy.46, pred[24576,256]{1,0:T(32,128)(4,1)S(1)} %bitcast_compare_fusion.2, bf16[64,24576]{1,0:T(8,128)(2,1)S(1)} %copy-done.1, pred[64]{0:T(512)(128)(4,1)S(1)} %compare_reduce_fusion.2), kind=kOutput, calls=%fused_computation.9.clone.1 | convolution fusion | flops 805322752 | bytes 9502788 | tf_op jit(solution)/shard_map/while/body/eval_jaxpr/dot_general | solution.py:25
  71.6 1.1 dynamic-slice_bitcast_fusion.2
  72.7 4.3 %bitcast_compare_fusion.2 = pred[24576,256]{1,0:T(32,128)(4,1)S(1)} fusion(s32[24576]{0:T(1024)S(1)} %bitcast.56, s32[96,256]{1,0:T(8,128)S(1)} %dynamic-slice_bitcast_fusion.2), kind=kLoop, calls=%fused_computation.6.clone.1 | loop fusion | flops 6291456 | bytes 6488064 | tf_op jit(solution)/shard_map/while/body/eval_jaxpr/eq | solution.py:23
  78.2 3.9 %fusion.21 = f32[8,256,64]{1,2,0:T(8,128)} fusion(f32[8,256,64]{1,2,0:T(8,128)} %get-tuple-element.111, s32[]{:T(128)S(6)} %copy.46, pred[24576,256]{1,0:T(32,128)(4,1)S(1)} %bitcast_compare_fusion.2, bf16[64,24576]{1,0:T(8,128)(2,1)S(1)} %copy-done.1, pred[64]{0:T(512)(128)(4,1)S(1)} %compare_reduce_fusion.2), kind=kOutput, calls=%fused_computation.9.clone.1 | convolution fusion | flops 805322752 | bytes 9502788 | tf_op jit(solution)/shard_map/while/body/eval_jaxpr/dot_general | solution.py:25
  82.2 1.1 dynamic-slice_bitcast_fusion.2
  83.3 4.3 %bitcast_compare_fusion.2 = pred[24576,256]{1,0:T(32,128)(4,1)S(1)} fusion(s32[24576]{0:T(1024)S(1)} %bitcast.56, s32[96,256]{1,0:T(8,128)S(1)} %dynamic-slice_bitcast_fusion.2), kind=kLoop, calls=%fused_computation.6.clone.1 | loop fusion | flops 6291456 | bytes 6488064 | tf_op jit(solution)/shard_map/while/body/eval_jaxpr/eq | solution.py:23
  88.8 3.9 %fusion.21 = f32[8,256,64]{1,2,0:T(8,128)} fusion(f32[8,256,64]{1,2,0:T(8,128)} %get-tuple-element.111, s32[]{:T(128)S(6)} %copy.46, pred[24576,256]{1,0:T(32,128)(4,1)S(1)} %bitcast_compare_fusion.2, bf16[64,24576]{1,0:T(8,128)(2,1)S(1)} %copy-done.1, pred[64]{0:T(512)(128)(4,1)S(1)} %compare_reduce_fusion.2), kind=kOutput, calls=%fused_computation.9.clone.1 | convolution fusion | flops 805322752 | bytes 9502788 | tf_op jit(solution)/shard_map/while/body/eval_jaxpr/dot_general | solution.py:25
  92.8 1.1 dynamic-slice_bitcast_fusion.2
  93.8 4.3 %bitcast_compare_fusion.2 = pred[24576,256]{1,0:T(32,128)(4,1)S(1)} fusion(s32[24576]{0:T(1024)S(1)} %bitcast.56, s32[96,256]{1,0:T(8,128)S(1)} %dynamic-slice_bitcast_fusion.2), kind=kLoop, calls=%fused_computation.6.clone.1 | loop fusion | flops 6291456 | bytes 6488064 | tf_op jit(solution)/shard_map/while/body/eval_jaxpr/eq | solution.py:23
  99.4 3.9 %fusion.21 = f32[8,256,64]{1,2,0:T(8,128)} fusion(f32[8,256,64]{1,2,0:T(8,128)} %get-tuple-element.111, s32[]{:T(128)S(6)} %copy.46, pred[24576,256]{1,0:T(32,128)(4,1)S(1)} %bitcast_compare_fusion.2, bf16[64,24576]{1,0:T(8,128)(2,1)S(1)} %copy-done.1, pred[64]{0:T(512)(128)(4,1)S(1)} %compare_reduce_fusion.2), kind=kOutput, calls=%fused_computation.9.clone.1 | convolution fusion | flops 805322752 | bytes 9502788 | tf_op jit(solution)/shard_map/while/body/eval_jaxpr/dot_general | solution.py:25
  103.4 1.1 dynamic-slice_bitcast_fusion.2
  104.4 4.3 %bitcast_compare_fusion.2 = pred[24576,256]{1,0:T(32,128)(4,1)S(1)} fusion(s32[24576]{0:T(1024)S(1)} %bitcast.56, s32[96,256]{1,0:T(8,128)S(1)} %dynamic-slice_bitcast_fusion.2), kind=kLoop, calls=%fused_computation.6.clone.1 | loop fusion | flops 6291456 | bytes 6488064 | tf_op jit(solution)/shard_map/while/body/eval_jaxpr/eq | solution.py:23
  110.0 3.9 %fusion.21 = f32[8,256,64]{1,2,0:T(8,128)} fusion(f32[8,256,64]{1,2,0:T(8,128)} %get-tuple-element.111, s32[]{:T(128)S(6)} %copy.46, pred[24576,256]{1,0:T(32,128)(4,1)S(1)} %bitcast_compare_fusion.2, bf16[64,24576]{1,0:T(8,128)(2,1)S(1)} %copy-done.1, pred[64]{0:T(512)(128)(4,1)S(1)} %compare_reduce_fusion.2), kind=kOutput, calls=%fused_computation.9.clone.1 | convolution fusion | flops 805322752 | bytes 9502788 | tf_op jit(solution)/shard_map/while/body/eval_jaxpr/dot_general | solution.py:25
  114.0 1.1 dynamic-slice_bitcast_fusion.2
  115.0 4.3 %bitcast_compare_fusion.2 = pred[24576,256]{1,0:T(32,128)(4,1)S(1)} fusion(s32[24576]{0:T(1024)S(1)} %bitcast.56, s32[96,256]{1,0:T(8,128)S(1)} %dynamic-slice_bitcast_fusion.2), kind=kLoop, calls=%fused_computation.6.clone.1 | loop fusion | flops 6291456 | bytes 6488064 | tf_op jit(solution)/shard_map/while/body/eval_jaxpr/eq | solution.py:23
  120.6 3.9 %fusion.21 = f32[8,256,64]{1,2,0:T(8,128)} fusion(f32[8,256,64]{1,2,0:T(8,128)} %get-tuple-element.111, s32[]{:T(128)S(6)} %copy.46, pred[24576,256]{1,0:T(32,128)(4,1)S(1)} %bitcast_compare_fusion.2, bf16[64,24576]{1,0:T(8,128)(2,1)S(1)} %copy-done.1, pred[64]{0:T(512)(128)(4,1)S(1)} %compare_reduce_fusion.2), kind=kOutput, calls=%fused_computation.9.clone.1 | convolution fusion | flops 805322752 | bytes 9502788 | tf_op jit(solution)/shard_map/while/body/eval_jaxpr/dot_general | solution.py:25
  124.6 1.1 dynamic-slice_bitcast_fusion.2
  125.6 4.3 %bitcast_compare_fusion.2 = pred[24576,256]{1,0:T(32,128)(4,1)S(1)} fusion(s32[24576]{0:T(1024)S(1)} %bitcast.56, s32[96,256]{1,0:T(8,128)S(1)} %dynamic-slice_bitcast_fusion.2), kind=kLoop, calls=%fused_computation.6.clone.1 | loop fusion | flops 6291456 | bytes 6488064 | tf_op jit(solution)/shard_map/while/body/eval_jaxpr/eq | solution.py:23
  131.2 3.9 %fusion.21 = f32[8,256,64]{1,2,0:T(8,128)} fusion(f32[8,256,64]{1,2,0:T(8,128)} %get-tuple-element.111, s32[]{:T(128)S(6)} %copy.46, pred[24576,256]{1,0:T(32,128)(4,1)S(1)} %bitcast_compare_fusion.2, bf16[64,24576]{1,0:T(8,128)(2,1)S(1)} %copy-done.1, pred[64]{0:T(512)(128)(4,1)S(1)} %compare_reduce_fusion.2), kind=kOutput, calls=%fused_computation.9.clone.1 | convolution fusion | flops 805322752 | bytes 9502788 | tf_op jit(solution)/shard_map/while/body/eval_jaxpr/dot_general | solution.py:25
  135.1 0.8 copy.30
  137.1 0.8 copy.32
  139.1 1.6 gather_fusion
  140.7 1.8 %reshape.147 = f32[32,4,768]{2,1,0:T(4,128)} reshape(f32[128,768]{1,0:T(8,128)} %gather_fusion) | data formatting | bytes 786432 | tf_op jit(solution)/shard_map/gather | solution.py:63
  142.5 1.2 multiply_reduce_fusion
  144.4 0.7 copy.33
  145.1 5.8 %all-to-all-start.2 = ((f32[32,1,4]{2,1,0:T(1,128)}), f32[32,1,4]{2,1,0:T(1,128)S(1)}, u32[]{:S(2)}, u32[]{:S(2)}) async-start(f32[32,1,4]{2,1,0:T(1,128)} %copy.33), calls=%async_computation.2 | async-start | bytes 32768 | tf_op jit(solution)/shard_map/all_to_all | solution.py:66
  151.6 6.5 %all-to-all-done.2 = f32[32,1,4]{2,1,0:T(1,128)S(1)} async-done(((f32[32,1,4]{2,1,0:T(1,128)}), f32[32,1,4]{2,1,0:T(1,128)S(1)}, u32[]{:S(2)}, u32[]{:S(2)}) %all-to-all-start.2) | async-done | bytes 544 | tf_op jit(solution)/shard_map/all_to_all | solution.py:66
  158.6 0.7 reduce.5
  159.4 1.2 gather_fusion.1
  (77 shorter events, 16.5 us)
Async XLA Ops:
  0.6 138.5 %copy-start = (f32[1024,768]{1,0:T(8,128)S(1)}, f32[1024,768]{1,0:T(8,128)}, u32[]{:S(2)}) copy-start(f32[1024,768]{1,0:T(8,128)} %param.13) | copy-start | bytes 9437188
  3.7 41.2 %copy-start.4 = (s32[128]{0:T(128)}, s32[128]{0:T(128)S(1)}, u32[]{:S(2)}) copy-start(s32[128]{0:T(128)S(1)} %fusion.10) | copy-start | bytes 1540
  5.4 39.5 %all-to-all-start = ((f32[32,1,4]{2,1,0:T(1,128)}), f32[32,1,4]{2,1,0:T(1,128)}, u32[]{:S(2)}, u32[]{:S(2)}) async-start(f32[32,1,4]{2,1,0:T(1,128)} %bitcast.4), calls=%async_computation | async-start | bytes 32768 | tf_op jit(solution)/shard_map/all_to_all | solution.py:60
  29.7 20.6 %copy-start.2 = (s32[64,8]{0,1:T(8,128)S(1)}, s32[64,8]{0,1:T(8,128)}, u32[]{:S(2)}) copy-start(s32[64,8]{0,1:T(8,128)} %param.12) | copy-start | bytes 6148
  44.8 97.7 %all-to-all-start.1 = ((f32[32,4,768]{2,1,0:T(4,128)}), f32[32,4,768]{2,1,0:T(4,128)S(1)}, u32[]{:S(2)}, u32[]{:S(2)}) async-start(f32[32,4,768]{2,1,0:T(4,128)} %reshape.135), calls=%async_computation.1 | async-start | bytes 786432 | tf_op jit(solution)/shard_map/all_to_all | solution.py:59
  50.3 6.7 %copy-start.1 = (bf16[64,24576]{1,0:T(8,128)(2,1)S(1)}, bf16[64,24576]{1,0:T(8,128)(2,1)}, u32[]{:S(2)}) copy-start(bf16[64,24576]{1,0:T(8,128)(2,1)} %get-tuple-element.122) | copy-start | bytes 9437188 | tf_op jit(solution)/shard_map/while
  60.9 6.7 %copy-start.1 = (bf16[64,24576]{1,0:T(8,128)(2,1)S(1)}, bf16[64,24576]{1,0:T(8,128)(2,1)}, u32[]{:S(2)}) copy-start(bf16[64,24576]{1,0:T(8,128)(2,1)} %get-tuple-element.122) | copy-start | bytes 9437188 | tf_op jit(solution)/shard_map/while
  71.5 6.7 %copy-start.1 = (bf16[64,24576]{1,0:T(8,128)(2,1)S(1)}, bf16[64,24576]{1,0:T(8,128)(2,1)}, u32[]{:S(2)}) copy-start(bf16[64,24576]{1,0:T(8,128)(2,1)} %get-tuple-element.122) | copy-start | bytes 9437188 | tf_op jit(solution)/shard_map/while
  82.1 6.7 %copy-start.1 = (bf16[64,24576]{1,0:T(8,128)(2,1)S(1)}, bf16[64,24576]{1,0:T(8,128)(2,1)}, u32[]{:S(2)}) copy-start(bf16[64,24576]{1,0:T(8,128)(2,1)} %get-tuple-element.122) | copy-start | bytes 9437188 | tf_op jit(solution)/shard_map/while
  92.7 6.7 %copy-start.1 = (bf16[64,24576]{1,0:T(8,128)(2,1)S(1)}, bf16[64,24576]{1,0:T(8,128)(2,1)}, u32[]{:S(2)}) copy-start(bf16[64,24576]{1,0:T(8,128)(2,1)} %get-tuple-element.122) | copy-start | bytes 9437188 | tf_op jit(solution)/shard_map/while
  103.3 6.7 %copy-start.1 = (bf16[64,24576]{1,0:T(8,128)(2,1)S(1)}, bf16[64,24576]{1,0:T(8,128)(2,1)}, u32[]{:S(2)}) copy-start(bf16[64,24576]{1,0:T(8,128)(2,1)} %get-tuple-element.122) | copy-start | bytes 9437188 | tf_op jit(solution)/shard_map/while
  113.9 6.7 %copy-start.1 = (bf16[64,24576]{1,0:T(8,128)(2,1)S(1)}, bf16[64,24576]{1,0:T(8,128)(2,1)}, u32[]{:S(2)}) copy-start(bf16[64,24576]{1,0:T(8,128)(2,1)} %get-tuple-element.122) | copy-start | bytes 9437188 | tf_op jit(solution)/shard_map/while
  124.5 6.7 %copy-start.1 = (bf16[64,24576]{1,0:T(8,128)(2,1)S(1)}, bf16[64,24576]{1,0:T(8,128)(2,1)}, u32[]{:S(2)}) copy-start(bf16[64,24576]{1,0:T(8,128)(2,1)} %get-tuple-element.122) | copy-start | bytes 9437188 | tf_op jit(solution)/shard_map/while
  135.9 0.6 copy-start.3
  145.1 13.0 %all-to-all-start.2 = ((f32[32,1,4]{2,1,0:T(1,128)}), f32[32,1,4]{2,1,0:T(1,128)S(1)}, u32[]{:S(2)}, u32[]{:S(2)}) async-start(f32[32,1,4]{2,1,0:T(1,128)} %copy.33), calls=%async_computation.2 | async-start | bytes 32768 | tf_op jit(solution)/shard_map/all_to_all | solution.py:66
where the time goes:
time: 162 us; the launch traced here: 161 us
  other arithmetic  45.8 us (28%)
  matrix products  38.9 us (24%)
  local copies, waits for them, and re-layouts  34.8 us (21%)
  starting transfers between devices  18.7 us (12%)
  blocking collectives  15.7 us (10%)
  waiting for transfers between devices  6.5 us (4%)
    eq x8, other arithmetic, one_list(): list_codes[:, None, :] == centres[None, :, None]  34.1 us
    dot_general x8, matrix products, one_list(): lax.dot_general(onehot, group_tables, (((0,), (1,)), ((), ())), preferred...  31.3 us
    all_gather x1, blocking collectives, per_device(): group_queries = lax.all_gather(queries, 'shard', axis=0, tiled=True)  15.7 us
    eq x8, local copies, waits for them, and re-layouts, one_list(): list_codes[:, None, :] == centres[None, :, None]  8.45 us
    dot_general x1, matrix products, build_tables(): jnp.einsum('qmd,mkd->qmk', pieces, codebook, precision=lax.Precision.HIGH...  7.55 us
    all_to_all x1, starting transfers between devices, rerank(): lax.all_to_all(send_ids, ('group', 'shard'), split_axis=0, concat_axis=0,...  7.45 us
    all_to_all x1, waiting for transfers between devices, rerank(): lax.all_to_all(scored, ('group', 'shard'), split_axis=0, concat_axis=0, t...  6.49 us
    all_to_all x1, starting transfers between devices, rerank(): lax.all_to_all(scored, ('group', 'shard'), split_axis=0, concat_axis=0, t...  5.83 us
  transfers between devices with their start and end apart: 3, of which 1 were waited for; matrix products, arithmetic and copies ran while one was open for 67% of the time, Pallas kernels for 0%

commit v1 on v0

--- a/solution.py
+++ b/solution.py
@@ -70,7 +70,11 @@
 
 def per_device(queries, codebook, pq_codes, probes, vectors, cand_owner, cand_row):
     first_list = lax.axis_index("shard") * pq_codes.shape[0]
-    group_queries = lax.all_gather(queries, "shard", axis=0, tiled=True)
+    count = lax.axis_size("shard")
+    repeats = [count if d == 0 else 1 for d in range(queries.ndim)]
+    group_queries = lax.all_to_all(
+        jnp.tile(queries, repeats), "shard", split_axis=0, concat_axis=0, tiled=True
+    )
     group_tables = build_tables(group_queries, codebook)
     pq_scores = score_lists(pq_codes, group_tables, probes, first_list)
     rerank_scores = rerank(queries, vectors, cand_owner, cand_row)

time: 162 us -> 157 us (0.969)
  starting transfers between devices: 18.7 us -> 12.6 us
  waiting for transfers between devices: 6.5 us -> 3.46 us
  other arithmetic: 45.8 us -> 48.4 us
    all_gather x1 -> x0, blocking collectives: 15.7 us -> none  [per_device(): group_queries = lax.all_gather(queries, 'shard', axis=0, tiled=True)]
    all_to_all x0 -> x1, blocking collectives: none -> 14.3 us  [rerank(): lax.all_to_all(send_ids, ('group', 'shard'), split_axis=0, concat_axis=0,...]
    all_to_all x1, waiting for transfers between devices: 6.49 us -> 0.01 us  [rerank(): lax.all_to_all(scored, ('group', 'shard'), split_axis=0, concat_axis=0, t...]
    reshape x0 -> x1, local copies, waits for them, and re-layouts: none -> 3.86 us  [build_tables(): pieces = query_rows.reshape(number, M, DS)]
    all_to_all x1, waiting for transfers between devices: 0.01 us -> 3.45 us  [per_device(): lax.all_to_all(jnp.tile(queries, repeats), 'shard', split_axis=0, concat_...]
    all_to_all x1, starting transfers between devices: 7.45 us -> 4.02 us  [per_device(): lax.all_to_all(jnp.tile(queries, repeats), 'shard', split_axis=0, concat_...]
    all_to_all x1, starting transfers between devices: 5.45 us -> 2.59 us  [rerank(): lax.all_to_all(send_rows, ('group', 'shard'), split_axis=0, concat_axis=0...]
    convert_element_type x1, local copies, waits for them, and re-layouts: 3.76 us -> 1.87 us  [build_tables(): return tables.reshape(number, M * KS).astype(jnp.bfloat16)]
  transfers between devices with their start and end apart: 3 -> 3, of which waited for: 1 -> 1; matrix products, arithmetic and copies ran while one was open for 67% -> 72% of each run, Pallas kernels for 0% -> 0%
where the time goes in v1:
time: 157 us; the launch traced here: 156 us
  other arithmetic  48.4 us (31%)
  matrix products  40 us (25%)
  local copies, waits for them, and re-layouts  36.3 us (23%)
  blocking collectives  14.3 us (9%)
  starting transfers between devices  12.6 us (8%)
  waiting for transfers between devices  3.46 us (2%)
    eq x8, other arithmetic, one_list(): list_codes[:, None, :] == centres[None, :, None]  34.6 us
    dot_general x8, matrix products, one_list(): lax.dot_general(onehot, group_tables, (((0,), (1,)), ((), ())), preferred...  31.3 us
    all_to_all x1, blocking collectives, rerank(): lax.all_to_all(send_ids, ('group', 'shard'), split_axis=0, concat_axis=0,...  14.3 us
    dot_general x1, matrix products, build_tables(): jnp.einsum('qmd,mkd->qmk', pieces, codebook, precision=lax.Precision.HIGH...  8.7 us
    eq x8, local copies, waits for them, and re-layouts, one_list(): list_codes[:, None, :] == centres[None, :, None]  7.25 us
    all_to_all x1, starting transfers between devices, rerank(): lax.all_to_all(scored, ('group', 'shard'), split_axis=0, concat_axis=0, t...  6.01 us
    reduce_or x8, other arithmetic, one_list(): probed = jnp.any(probes == list_id, axis=1)  5.11 us
    dynamic_slice x8, local copies, waits for them, and re-layouts, score_lists(): return lax.map(one_list, (pq_codes, list_ids))  4.8 us
  transfers between devices with their start and end apart: 3, of which 1 were waited for; matrix products, arithmetic and copies ran while one was open for 72% of the time, Pallas kernels for 0%

profile of v1, /device:TPU:0, one launch (start us, length us, event | category | flops | bytes accessed | tf_op | source)
XLA Modules:
  0.0 156.1 jit_solution(7410046930991553723)
XLA Ops:
  0.6 0.8 broadcast_multiply_fusion
  1.5 0.9 eq.43
  4.2 1.0 scatter_custom_fusion
  5.3 14.3 %all_to_all.29 = f32[32,1,4]{2,1,0:T(1,128)S(1)} all-to-all(f32[32,1,4]{2,1,0:T(1,128)S(1)} %bitcast.54), channel_id=1, replica_groups=mesh['group'=4,'shard'=8] {'group','shard'}, dimensions={0} | all-to-all | bytes 1024 | tf_op jit(solution)/shard_map/all_to_all | solution.py:60
  19.6 1.4 tile.2
  21.1 4.0 %all-to-all-start = ((f32[8,8,768]{2,1,0:T(8,128)}), f32[8,8,768]{2,1,0:T(8,128)}, u32[]{:S(2)}, u32[]{:S(2)}) async-start(f32[8,8,768]{2,1,0:T(8,128)} %tile.2), calls=%async_computation | async-start | bytes 393216 | tf_op jit(solution)/shard_map/all_to_all | solution.py:75
  25.7 3.4 %scatter_custom_fusion.1 = f32[128,768]{1,0:T(8,128)S(1)} fusion(s32[128]{0:T(128)} %copy-done.4, f32[8,768]{1,0:T(8,128)} %param.9, s32[1024]{0:T(1024)} %pad_clamp_fusion.2, f32[]{:T(128)} %constant.28.clone.1), kind=kCustom, calls=%fused_computation.17 | custom fusion | bytes 393728 | tf_op jit(solution)/shard_map/scatter | solution.py:50
  29.1 0.9 reshape.143
  29.9 3.5 %all-to-all-done = f32[8,8,768]{2,1,0:T(8,128)} async-done(((f32[8,8,768]{2,1,0:T(8,128)}), f32[8,8,768]{2,1,0:T(8,128)}, u32[]{:S(2)}, u32[]{:S(2)}) %all-to-all-start) | async-done | bytes 196640 | tf_op jit(solution)/shard_map/all_to_all | solution.py:75
  33.4 2.6 %all-to-all-start.2 = ((f32[32,4,768]{2,1,0:T(4,128)}), f32[32,4,768]{2,1,0:T(4,128)S(1)}, u32[]{:S(2)}, u32[]{:S(2)}) async-start(f32[32,4,768]{2,1,0:T(4,128)} %reshape.143), calls=%async_computation.2 | async-start | bytes 786432 | tf_op jit(solution)/shard_map/all_to_all | solution.py:59
  36.5 1.2 pad_clamp_fusion
  38.4 1.3 compare_select_fusion
  39.7 0.8 copy.32
  41.7 1.5 gather_fusion
  43.2 1.8 %reshape.155 = f32[32,4,768]{2,1,0:T(4,128)} reshape(f32[128,768]{1,0:T(8,128)} %gather_fusion) | data formatting | bytes 786432 | tf_op jit(solution)/shard_map/gather | solution.py:63
  45.1 3.9 %reshape.142 = f32[64,96,8]{2,1,0:T(8,128)} reshape(f32[8,8,768]{2,1,0:T(8,128)} %all-to-all-done) | data formatting | bytes 393216 | tf_op jit(solution)/shard_map/reshape | solution.py:13
  48.9 8.7 %convert_bitcast_fusion = bf16[96,8,8,256]{3,2,1,0:T(8,128)(2,1)S(1)} fusion(f32[96,256,8]{1,2,0:T(8,128)} %param.10, f32[64,96,8]{2,1,0:T(8,128)} %reshape.142), kind=kOutput, calls=%fused_computation.15 | convolution fusion | flops 152567808 | bytes 4128768 | tf_op jit(solution)/shard_map/qmd,mkd->qmk/dot_general | solution.py:14
  57.7 1.9 %copy.40 = bf16[96,8,8,256]{3,2,0,1:T(8,128)(2,1)} copy(bf16[96,8,8,256]{3,2,1,0:T(8,128)(2,1)S(1)} %convert_bitcast_fusion) | data formatting | bytes 6291456 | tf_op jit(solution)/shard_map/convert_element_type | solution.py:15
  59.6 1.8 %multiply_reduce_fusion = f32[32,4]{1,0:T(8,128)} fusion(f32[32,4,768]{2,1,0:T(4,128)S(1)} %all-to-all-done.2, f32[32,4,768]{2,1,0:T(4,128)} %reshape.155), kind=kLoop, calls=%fused_computation.16 | loop fusion | flops 196480 | bytes 786944
  61.3 0.8 copy.38
  62.8 6.0 %all-to-all-start.3 = ((f32[32,1,4]{2,1,0:T(1,128)}), f32[32,1,4]{2,1,0:T(1,128)S(1)}, u32[]{:S(2)}, u32[]{:S(2)}) async-start(f32[32,1,4]{2,1,0:T(1,128)} %copy.33), calls=%async_computation.3 | async-start | bytes 32768 | tf_op jit(solution)/shard_map/all_to_all | solution.py:66
  68.9 83.8 %while.11 = (s32[]{:T(128)}, f32[8,256,64]{1,2,0:T(8,128)}, s32[8]{0:T(128)S(1)}, s32[64,8]{0,1:T(8,128)S(1)}, s32[8,96,256]{2,1,0:T(8,128)}, /*index=5*/bf16[64,24576]{1,0:T(8,128)(2,1)}, s32[]{:T(128)}) while((s32[]{:T(128)}, f32[8,256,64]{1,2,0:T(8,128)}, s32[8]{0:T(128)S(1)}, s32[64,8]{0,1:T(8,128)S(1)}, ...), condition=%wide.region_2.3_spmd.clone, body=%wide.region_0.2_spmd.clone.sunk | while | flops 811615168 | bytes 29067528 | solution.py:32
  68.9 0.9 dynamic-slice_bitcast_fusion.2
  69.9 4.3 %bitcast_compare_fusion.2 = pred[24576,256]{1,0:T(32,128)(4,1)S(1)} fusion(s32[24576]{0:T(1024)S(1)} %bitcast.53, s32[96,256]{1,0:T(8,128)S(1)} %dynamic-slice_bitcast_fusion.2), kind=kLoop, calls=%fused_computation.6.clone.1 | loop fusion | flops 6291456 | bytes 6488064 | tf_op jit(solution)/shard_map/while/body/eval_jaxpr/eq | solution.py:23
  75.4 3.9 %fusion.24 = f32[8,256,64]{1,2,0:T(8,128)} fusion(f32[8,256,64]{1,2,0:T(8,128)} %get-tuple-element.111, s32[]{:T(128)S(6)} %copy.50, pred[24576,256]{1,0:T(32,128)(4,1)S(1)} %bitcast_compare_fusion.2, bf16[64,24576]{1,0:T(8,128)(2,1)S(1)} %copy-done.1, pred[64]{0:T(512)(128)(4,1)S(1)} %compare_reduce_fusion.2), kind=kOutput, calls=%fused_computation.9.clone.1 | convolution fusion | flops 805322752 | bytes 9502788 | tf_op jit(solution)/shard_map/while/body/eval_jaxpr/dot_general | solution.py:25
  79.4 0.9 dynamic-slice_bitcast_fusion.2
  80.3 4.3 %bitcast_compare_fusion.2 = pred[24576,256]{1,0:T(32,128)(4,1)S(1)} fusion(s32[24576]{0:T(1024)S(1)} %bitcast.53, s32[96,256]{1,0:T(8,128)S(1)} %dynamic-slice_bitcast_fusion.2), kind=kLoop, calls=%fused_computation.6.clone.1 | loop fusion | flops 6291456 | bytes 6488064 | tf_op jit(solution)/shard_map/while/body/eval_jaxpr/eq | solution.py:23
  85.9 3.9 %fusion.24 = f32[8,256,64]{1,2,0:T(8,128)} fusion(f32[8,256,64]{1,2,0:T(8,128)} %get-tuple-element.111, s32[]{:T(128)S(6)} %copy.50, pred[24576,256]{1,0:T(32,128)(4,1)S(1)} %bitcast_compare_fusion.2, bf16[64,24576]{1,0:T(8,128)(2,1)S(1)} %copy-done.1, pred[64]{0:T(512)(128)(4,1)S(1)} %compare_reduce_fusion.2), kind=kOutput, calls=%fused_computation.9.clone.1 | convolution fusion | flops 805322752 | bytes 9502788 | tf_op jit(solution)/shard_map/while/body/eval_jaxpr/dot_general | solution.py:25
  89.9 0.9 dynamic-slice_bitcast_fusion.2
  90.8 4.3 %bitcast_compare_fusion.2 = pred[24576,256]{1,0:T(32,128)(4,1)S(1)} fusion(s32[24576]{0:T(1024)S(1)} %bitcast.53, s32[96,256]{1,0:T(8,128)S(1)} %dynamic-slice_bitcast_fusion.2), kind=kLoop, calls=%fused_computation.6.clone.1 | loop fusion | flops 6291456 | bytes 6488064 | tf_op jit(solution)/shard_map/while/body/eval_jaxpr/eq | solution.py:23
  96.4 3.9 %fusion.24 = f32[8,256,64]{1,2,0:T(8,128)} fusion(f32[8,256,64]{1,2,0:T(8,128)} %get-tuple-element.111, s32[]{:T(128)S(6)} %copy.50, pred[24576,256]{1,0:T(32,128)(4,1)S(1)} %bitcast_compare_fusion.2, bf16[64,24576]{1,0:T(8,128)(2,1)S(1)} %copy-done.1, pred[64]{0:T(512)(128)(4,1)S(1)} %compare_reduce_fusion.2), kind=kOutput, calls=%fused_computation.9.clone.1 | convolution fusion | flops 805322752 | bytes 9502788 | tf_op jit(solution)/shard_map/while/body/eval_jaxpr/dot_general | solution.py:25
  100.4 0.9 dynamic-slice_bitcast_fusion.2
  101.3 4.3 %bitcast_compare_fusion.2 = pred[24576,256]{1,0:T(32,128)(4,1)S(1)} fusion(s32[24576]{0:T(1024)S(1)} %bitcast.53, s32[96,256]{1,0:T(8,128)S(1)} %dynamic-slice_bitcast_fusion.2), kind=kLoop, calls=%fused_computation.6.clone.1 | loop fusion | flops 6291456 | bytes 6488064 | tf_op jit(solution)/shard_map/while/body/eval_jaxpr/eq | solution.py:23
  106.8 3.9 %fusion.24 = f32[8,256,64]{1,2,0:T(8,128)} fusion(f32[8,256,64]{1,2,0:T(8,128)} %get-tuple-element.111, s32[]{:T(128)S(6)} %copy.50, pred[24576,256]{1,0:T(32,128)(4,1)S(1)} %bitcast_compare_fusion.2, bf16[64,24576]{1,0:T(8,128)(2,1)S(1)} %copy-done.1, pred[64]{0:T(512)(128)(4,1)S(1)} %compare_reduce_fusion.2), kind=kOutput, calls=%fused_computation.9.clone.1 | convolution fusion | flops 805322752 | bytes 9502788 | tf_op jit(solution)/shard_map/while/body/eval_jaxpr/dot_general | solution.py:25
  110.8 0.9 dynamic-slice_bitcast_fusion.2
  111.7 4.3 %bitcast_compare_fusion.2 = pred[24576,256]{1,0:T(32,128)(4,1)S(1)} fusion(s32[24576]{0:T(1024)S(1)} %bitcast.53, s32[96,256]{1,0:T(8,128)S(1)} %dynamic-slice_bitcast_fusion.2), kind=kLoop, calls=%fused_computation.6.clone.1 | loop fusion | flops 6291456 | bytes 6488064 | tf_op jit(solution)/shard_map/while/body/eval_jaxpr/eq | solution.py:23
  117.3 3.9 %fusion.24 = f32[8,256,64]{1,2,0:T(8,128)} fusion(f32[8,256,64]{1,2,0:T(8,128)} %get-tuple-element.111, s32[]{:T(128)S(6)} %copy.50, pred[24576,256]{1,0:T(32,128)(4,1)S(1)} %bitcast_compare_fusion.2, bf16[64,24576]{1,0:T(8,128)(2,1)S(1)} %copy-done.1, pred[64]{0:T(512)(128)(4,1)S(1)} %compare_reduce_fusion.2), kind=kOutput, calls=%fused_computation.9.clone.1 | convolution fusion | flops 805322752 | bytes 9502788 | tf_op jit(solution)/shard_map/while/body/eval_jaxpr/dot_general | solution.py:25
  121.3 0.9 dynamic-slice_bitcast_fusion.2
  122.2 4.3 %bitcast_compare_fusion.2 = pred[24576,256]{1,0:T(32,128)(4,1)S(1)} fusion(s32[24576]{0:T(1024)S(1)} %bitcast.53, s32[96,256]{1,0:T(8,128)S(1)} %dynamic-slice_bitcast_fusion.2), kind=kLoop, calls=%fused_computation.6.clone.1 | loop fusion | flops 6291456 | bytes 6488064 | tf_op jit(solution)/shard_map/while/body/eval_jaxpr/eq | solution.py:23
  127.8 3.9 %fusion.24 = f32[8,256,64]{1,2,0:T(8,128)} fusion(f32[8,256,64]{1,2,0:T(8,128)} %get-tuple-element.111, s32[]{:T(128)S(6)} %copy.50, pred[24576,256]{1,0:T(32,128)(4,1)S(1)} %bitcast_compare_fusion.2, bf16[64,24576]{1,0:T(8,128)(2,1)S(1)} %copy-done.1, pred[64]{0:T(512)(128)(4,1)S(1)} %compare_reduce_fusion.2), kind=kOutput, calls=%fused_computation.9.clone.1 | convolution fusion | flops 805322752 | bytes 9502788 | tf_op jit(solution)/shard_map/while/body/eval_jaxpr/dot_general | solution.py:25
  131.8 0.9 dynamic-slice_bitcast_fusion.2
  132.7 4.3 %bitcast_compare_fusion.2 = pred[24576,256]{1,0:T(32,128)(4,1)S(1)} fusion(s32[24576]{0:T(1024)S(1)} %bitcast.53, s32[96,256]{1,0:T(8,128)S(1)} %dynamic-slice_bitcast_fusion.2), kind=kLoop, calls=%fused_computation.6.clone.1 | loop fusion | flops 6291456 | bytes 6488064 | tf_op jit(solution)/shard_map/while/body/eval_jaxpr/eq | solution.py:23
  138.3 3.9 %fusion.24 = f32[8,256,64]{1,2,0:T(8,128)} fusion(f32[8,256,64]{1,2,0:T(8,128)} %get-tuple-element.111, s32[]{:T(128)S(6)} %copy.50, pred[24576,256]{1,0:T(32,128)(4,1)S(1)} %bitcast_compare_fusion.2, bf16[64,24576]{1,0:T(8,128)(2,1)S(1)} %copy-done.1, pred[64]{0:T(512)(128)(4,1)S(1)} %compare_reduce_fusion.2), kind=kOutput, calls=%fused_computation.9.clone.1 | convolution fusion | flops 805322752 | bytes 9502788 | tf_op jit(solution)/shard_map/while/body/eval_jaxpr/dot_general | solution.py:25
  142.2 0.9 dynamic-slice_bitcast_fusion.2
  143.1 4.3 %bitcast_compare_fusion.2 = pred[24576,256]{1,0:T(32,128)(4,1)S(1)} fusion(s32[24576]{0:T(1024)S(1)} %bitcast.53, s32[96,256]{1,0:T(8,128)S(1)} %dynamic-slice_bitcast_fusion.2), kind=kLoop, calls=%fused_computation.6.clone.1 | loop fusion | flops 6291456 | bytes 6488064 | tf_op jit(solution)/shard_map/while/body/eval_jaxpr/eq | solution.py:23
  148.7 3.9 %fusion.24 = f32[8,256,64]{1,2,0:T(8,128)} fusion(f32[8,256,64]{1,2,0:T(8,128)} %get-tuple-element.111, s32[]{:T(128)S(6)} %copy.50, pred[24576,256]{1,0:T(32,128)(4,1)S(1)} %bitcast_compare_fusion.2, bf16[64,24576]{1,0:T(8,128)(2,1)S(1)} %copy-done.1, pred[64]{0:T(512)(128)(4,1)S(1)} %compare_reduce_fusion.2), kind=kOutput, calls=%fused_computation.9.clone.1 | convolution fusion | flops 805322752 | bytes 9502788 | tf_op jit(solution)/shard_map/while/body/eval_jaxpr/dot_general | solution.py:25
  153.2 0.7 reduce.5
  154.1 1.4 gather_fusion.1
  (80 shorter events, 17.5 us)
Async XLA Ops:
  0.6 41.1 %copy-start = (f32[1024,768]{1,0:T(8,128)S(1)}, f32[1024,768]{1,0:T(8,128)}, u32[]{:S(2)}) copy-start(f32[1024,768]{1,0:T(8,128)} %param.13) | copy-start | bytes 9437188
  3.7 0.6 copy-start.4
  21.1 12.3 %all-to-all-start = ((f32[8,8,768]{2,1,0:T(8,128)}), f32[8,8,768]{2,1,0:T(8,128)}, u32[]{:S(2)}, u32[]{:S(2)}) async-start(f32[8,8,768]{2,1,0:T(8,128)} %tile.2), calls=%async_computation | async-start | bytes 393216 | tf_op jit(solution)/shard_map/all_to_all | solution.py:75
  33.4 26.2 %all-to-all-start.2 = ((f32[32,4,768]{2,1,0:T(4,128)}), f32[32,4,768]{2,1,0:T(4,128)S(1)}, u32[]{:S(2)}, u32[]{:S(2)}) async-start(f32[32,4,768]{2,1,0:T(4,128)} %reshape.143), calls=%async_computation.2 | async-start | bytes 786432 | tf_op jit(solution)/shard_map/all_to_all | solution.py:59
  57.7 4.5 %copy-start.3 = (f32[32,1,4]{0,2,1:T(4,128)S(1)}, f32[32,1,4]{0,2,1:T(4,128)}, u32[]{:S(2)}) copy-start(f32[32,1,4]{0,2,1:T(4,128)} %copy.30) | copy-start | bytes 1540
  57.7 11.2 %copy-start.2 = (s32[64,8]{0,1:T(8,128)S(1)}, s32[64,8]{0,1:T(8,128)}, u32[]{:S(2)}) copy-start(s32[64,8]{0,1:T(8,128)} %param.12) | copy-start | bytes 6148
  57.7 11.2 %copy-start.5 = (s32[8]{0:T(128)S(1)}, s32[8]{0:T(128)}, u32[]{:S(2)}) copy-start(s32[8]{0:T(128)} %iota_add_fusion) | copy-start | bytes 100
  62.8 89.8 %all-to-all-start.3 = ((f32[32,1,4]{2,1,0:T(1,128)}), f32[32,1,4]{2,1,0:T(1,128)S(1)}, u32[]{:S(2)}, u32[]{:S(2)}) async-start(f32[32,1,4]{2,1,0:T(1,128)} %copy.33), calls=%async_computation.3 | async-start | bytes 32768 | tf_op jit(solution)/shard_map/all_to_all | solution.py:66
  69.8 5.6 %copy-start.1 = (bf16[64,24576]{1,0:T(8,128)(2,1)S(1)}, bf16[64,24576]{1,0:T(8,128)(2,1)}, u32[]{:S(2)}) copy-start(bf16[64,24576]{1,0:T(8,128)(2,1)} %get-tuple-element.122) | copy-start | bytes 9437188 | tf_op jit(solution)/shard_map/while
  80.3 5.6 %copy-start.1 = (bf16[64,24576]{1,0:T(8,128)(2,1)S(1)}, bf16[64,24576]{1,0:T(8,128)(2,1)}, u32[]{:S(2)}) copy-start(bf16[64,24576]{1,0:T(8,128)(2,1)} %get-tuple-element.122) | copy-start | bytes 9437188 | tf_op jit(solution)/shard_map/while
  90.8 5.6 %copy-start.1 = (bf16[64,24576]{1,0:T(8,128)(2,1)S(1)}, bf16[64,24576]{1,0:T(8,128)(2,1)}, u32[]{:S(2)}) copy-start(bf16[64,24576]{1,0:T(8,128)(2,1)} %get-tuple-element.122) | copy-start | bytes 9437188 | tf_op jit(solution)/shard_map/while
  101.3 5.6 %copy-start.1 = (bf16[64,24576]{1,0:T(8,128)(2,1)S(1)}, bf16[64,24576]{1,0:T(8,128)(2,1)}, u32[]{:S(2)}) copy-start(bf16[64,24576]{1,0:T(8,128)(2,1)} %get-tuple-element.122) | copy-start | bytes 9437188 | tf_op jit(solution)/shard_map/while
  111.7 5.6 %copy-start.1 = (bf16[64,24576]{1,0:T(8,128)(2,1)S(1)}, bf16[64,24576]{1,0:T(8,128)(2,1)}, u32[]{:S(2)}) copy-start(bf16[64,24576]{1,0:T(8,128)(2,1)} %get-tuple-element.122) | copy-start | bytes 9437188 | tf_op jit(solution)/shard_map/while
  122.2 5.6 %copy-start.1 = (bf16[64,24576]{1,0:T(8,128)(2,1)S(1)}, bf16[64,24576]{1,0:T(8,128)(2,1)}, u32[]{:S(2)}) copy-start(bf16[64,24576]{1,0:T(8,128)(2,1)} %get-tuple-element.122) | copy-start | bytes 9437188 | tf_op jit(solution)/shard_map/while
  132.7 5.6 %copy-start.1 = (bf16[64,24576]{1,0:T(8,128)(2,1)S(1)}, bf16[64,24576]{1,0:T(8,128)(2,1)}, u32[]{:S(2)}) copy-start(bf16[64,24576]{1,0:T(8,128)(2,1)} %get-tuple-element.122) | copy-start | bytes 9437188 | tf_op jit(solution)/shard_map/while
  143.1 5.6 %copy-start.1 = (bf16[64,24576]{1,0:T(8,128)(2,1)S(1)}, bf16[64,24576]{1,0:T(8,128)(2,1)}, u32[]{:S(2)}) copy-start(bf16[64,24576]{1,0:T(8,128)(2,1)} %get-tuple-element.122) | copy-start | bytes 9437188 | tf_op jit(solution)/shard_map/while
